TPU v7x, 32 devices: a whole 2x2x4 slice. The times are simulated.
32 devices in a mesh: slab: 4 (over z), tile: 8 (over y, x, core).
Axes of the slice: x: 2, y: 2, z: 4, core: 2. Of those that a mesh axis runs over, the one named last changes fastest.
Arguments:
- coarse: bfloat16 [192, 16, 32, 64], P(None, 'slab', 'tile'), may hold values from -6 to 6
- up_weight: bfloat16 [3, 3, 96, 192], replicated, may hold values from -0.15625 to 0.15625
- up_bias: float32 [96], replicated, may hold values from -3 to 3
- gain_one: float32 [96], replicated, may hold values from 0.1 to 1.9
- conv_one: bfloat16 [3, 3, 96, 288], replicated, may hold values from -0.125 to 0.125
- bias_one: float32 [96], replicated, may hold values from -3 to 3
- gain_two: float32 [96], replicated, may hold values from 0.1 to 1.9
- conv_two: bfloat16 [3, 3, 96, 288], replicated, may hold values from -0.125 to 0.125
- bias_two: float32 [96], replicated, may hold values from -3 to 3
Outputs:
- decoded: bfloat16 [96, 16, 64, 128], P(None, 'slab', 'tile')
All inputs are finite; a program needn't handle non-finite values.
Results may differ from a plain program's by a relative error of at most 0.009.
Values may be sent and summed in bfloat16 or wider, within the bound.
A program may use at most 64 MiB of HBM per device.

v0:
```python
import functools

import jax
import jax.numpy as jnp
from jax import lax
from jax.experimental import pallas as pl
from jax.experimental.pallas import tpu as pltpu
from jax.sharding import PartitionSpec as P

MESH = pl.DeviceIdType.MESH
F32 = jnp.float32
BF16 = jnp.bfloat16


def body(slabs, tiles, coarse, wu, w1, w2, vecs, out, cbuf, part, ups, x1, acc1, x2, acc2,
         near_send, near_recv, far_send, far_recv, hop_send, hop_recv):
    frames, _, _, cols = coarse.shape
    chans = out.shape[2]
    rows = out.shape[1]
    s = lax.axis_index("slab")
    t = lax.axis_index("tile")
    has_up, has_down = t > 0, t < tiles - 1
    has_prev, has_next = s > 0, s < slabs - 1
    sides = ((has_up, {"tile": t - 1}), (has_down, {"tile": t + 1}), (has_prev, {"slab": s - 1}), (has_next, {"slab": s + 1}))

    def remote(src, dst, send, recv, who):
        return pltpu.make_async_remote_copy(
            src_ref=src, dst_ref=dst, send_sem=send, recv_sem=recv, device_id=who, device_id_type=MESH)

    barrier = pltpu.get_barrier_semaphore()
    for there, who in sides:
        @pl.when(there)
        def _():
            pl.semaphore_signal(barrier, inc=1, device_id=who, device_id_type=MESH)
    pl.semaphore_wait(barrier, sum(there.astype(jnp.int32) for there, _ in sides))

    to_up = remote(coarse.at[:, 0], cbuf.at[pl.ds(frames, frames), 3], near_send.at[0], near_recv.at[0], {"tile": t - 1})
    to_down = remote(coarse.at[:, 1], cbuf.at[pl.ds(frames, frames), 0], near_send.at[1], near_recv.at[1], {"tile": t + 1})
    far = [remote(coarse.at[f], cbuf.at[f, pl.ds(1, 2)], far_send.at[f], far_recv.at[f], {"slab": s + 1}) for f in range(frames)]
    hop_up = [remote(cbuf.at[f, 1], cbuf.at[f, 3], hop_send.at[f, 0], hop_recv.at[f, 0], {"tile": t - 1}) for f in range(frames)]
    hop_down = [remote(cbuf.at[f, 2], cbuf.at[f, 0], hop_send.at[f, 1], hop_recv.at[f, 1], {"tile": t + 1}) for f in range(frames)]

    pl.when(has_up)(to_up.start)
    pl.when(has_down)(to_down.start)
    for f in reversed(range(frames)):
        pl.when(has_next)(far[f].start)

    for f in range(frames):
        cbuf[frames + f, 1] = coarse[f, 0]
        cbuf[frames + f, 2] = coarse[f, 1]

    rim = jnp.zeros(cbuf.shape[2:], BF16)

    @pl.when(jnp.logical_not(has_up))
    def _():
        for f in range(frames):
            cbuf[frames + f, 0] = rim

    @pl.when(jnp.logical_not(has_down))
    def _():
        for f in range(frames):
            cbuf[frames + f, 3] = rim

    @pl.when(jnp.logical_or(jnp.logical_not(has_prev), jnp.logical_not(has_up)))
    def _():
        for f in range(frames):
            cbuf[f, 0] = rim

    @pl.when(jnp.logical_or(jnp.logical_not(has_prev), jnp.logical_not(has_down)))
    def _():
        for f in range(frames):
            cbuf[f, 3] = rim

    @pl.when(jnp.logical_not(has_prev))
    def _():
        for f in range(frames):
            cbuf[f, 1] = rim
            cbuf[f, 2] = rim

    half = cols // 2
    lane = lax.broadcasted_iota(jnp.int32, (cols, cols), 0)
    col = lax.broadcasted_iota(jnp.int32, (cols, cols), 1)
    pieces = []
    for j in range(2):
        for b in range(3):
            at = col + (b - 1)
            inside = jnp.logical_and(at >= 0, at < cols)
            hit = jnp.logical_and(inside, lane == j * half + lax.shift_right_arithmetic(at, 1))
            pieces.append(jnp.where(hit, 1.0, 0.0).astype(BF16))
    spread = jnp.concatenate(pieces, axis=1)

    row_col = lax.broadcasted_iota(jnp.int32, (chans, cols), 1)
    first_col = row_col == 0
    last_col = row_col == cols - 1

    def norm_act(values, gain):
        meansq = jnp.mean(values * values, axis=0, keepdims=True)
        y = values * lax.rsqrt(meansq + 1e-06) * gain
        return y / (1.0 + jnp.exp(-y))

    def put(ref, f, r, act):
        ref[f, r, pl.ds(0, chans)] = jnp.where(first_col, 0.0, pltpu.roll(act, 1, 1)).astype(BF16)
        ref[f, r, pl.ds(chans, chans)] = act.astype(BF16)
        ref[f, r, pl.ds(2 * chans, chans)] = jnp.where(last_col, 0.0, pltpu.roll(act, cols - 1, 1)).astype(BF16)

    top_keep = jnp.where(has_up, 1.0, 0.0)
    bottom_keep = jnp.where(has_down, 1.0, 0.0)
    past_keep = jnp.where(has_prev, 1.0, 0.0)

    def row_keep(r, low, high):
        return jnp.where(r < low, top_keep, jnp.where(r >= high, bottom_keep, 1.0))

    def upsample(f):
        def expand(pair, _):
            wide = jnp.dot(cbuf[f, pair], spread, preferred_element_type=F32).astype(BF16)
            stacks = []
            for j in range(2):
                stacks.append(jnp.concatenate([wide[:, (3 * j + b) * cols:(3 * j + b + 1) * cols] for b in range(3)], axis=0))
            got = jnp.dot(wu[...], jnp.concatenate(stacks, axis=1), preferred_element_type=F32)
            part[2 * pair] = got[:, :cols]
            part[2 * pair + 1] = got[:, cols:]
            return _
        lax.fori_loop(0, 4, expand, 0)

        def finish(i, _):
            even = part[i, pl.ds(chans, chans)] + part[i - 1, pl.ds(3 * chans, chans)]
            odd = part[i, pl.ds(2 * chans, chans)] + part[i + 1, pl.ds(0, chans)]
            for j, total in enumerate((even, odd)):
                r = 2 * (i - 1) + j
                value = (total + vecs[0]).astype(BF16)
                if f >= frames:
                    ups[f - frames, r] = value
                act = norm_act(value.astype(F32), vecs[1])
                keep = row_keep(r, 2, rows + 2)
                if f < frames:
                    keep = keep * past_keep
                put(x1, f, r, act * keep)
            return _
        lax.fori_loop(1, 7, finish, 0)

    def conv(x, w, acc, f, last, pairs):
        taps = [tap for tap in range(3) if 0 <= f - tap <= last]
        lo, hi = taps[0], taps[-1] + 1

        def step(p, _):
            r = 2 * p
            lines = [x[f, r + a] for a in range(4)]
            rhs = jnp.concatenate([jnp.concatenate([lines[a], lines[a + 1]], axis=1) for a in range(3)], axis=0)
            got = jnp.dot(w[pl.ds(lo * chans, (hi - lo) * chans)], rhs, preferred_element_type=F32)
            for tap in taps:
                mine = got[(tap - lo) * chans:(tap - lo + 1) * chans]
                acc[f - tap, r] = acc[f - tap, r] + mine[:, :cols]
                acc[f - tap, r + 1] = acc[f - tap, r + 1] + mine[:, cols:]
            return _
        lax.fori_loop(0, pairs, step, 0)

    def second(n):
        def step(r, _):
            act = norm_act(acc1[n, r], vecs[3])
            keep = row_keep(r, 1, rows + 1)
            if n < 2:
                keep = keep * past_keep
            put(x2, n, r, act * keep)
            return _
        lax.fori_loop(0, rows + 2, step, 0)

    mids = frames + 2
    for n in range(mids):
        def fill(r, _):
            acc1[n, r] = vecs[2]
            return _
        lax.fori_loop(0, rows + 2, fill, 0)

    pl.when(has_down)(to_up.wait_recv)
    pl.when(has_up)(to_down.wait_recv)

    def relay(f):
        @pl.when(has_prev)
        def _():
            far[f].wait_recv()
            pl.when(has_up)(hop_up[f].start)
            pl.when(has_down)(hop_down[f].start)

    def landed(f):
        @pl.when(has_prev)
        def _():
            pl.when(has_down)(hop_up[f].wait_recv)
            pl.when(has_up)(hop_down[f].wait_recv)

    for f in reversed(range(frames, 2 * frames)):
        upsample(f)
    for f in reversed(range(frames, 2 * frames)):
        relay(f - frames)
        conv(x1, w1, acc1, f, mids - 1, (rows + 2) // 2)
    for f in reversed(range(frames)):
        landed(f)
        upsample(f)
        conv(x1, w1, acc1, f, mids - 1, (rows + 2) // 2)
    for n in range(mids):
        second(n)

    for n in range(frames):
        def begin(r, _):
            acc2[n, r] = ups[n, r + 2].astype(F32) + vecs[4]
            return _
        lax.fori_loop(0, rows, begin, 0)
    for f in reversed(range(mids)):
        conv(x2, w2, acc2, f, frames - 1, rows // 2)
    for n in range(frames):
        def end(r, _):
            out[n, r] = acc2[n, r].astype(BF16)
            return _
        lax.fori_loop(0, rows, end, 0)

    pl.when(has_up)(to_up.wait_send)
    pl.when(has_down)(to_down.wait_send)
    for f in range(frames):
        pl.when(has_next)(far[f].wait_send)
        pl.when(jnp.logical_and(has_prev, has_up))(hop_up[f].wait_send)
        pl.when(jnp.logical_and(has_prev, has_down))(hop_down[f].wait_send)


def shards(slabs, tiles, coarse, up_weight, up_bias, gain_one, conv_one, bias_one, gain_two, conv_two, bias_two):
    deep, frames, lines, half = coarse.shape
    chans = up_weight.shape[2]
    rows, cols = 2 * lines, 2 * half
    packed = coarse.transpose(1, 2, 0, 3).reshape(frames, lines // 2, 2, deep, half)
    packed = packed.transpose(0, 1, 3, 2, 4).reshape(frames, lines // 2, deep, cols)
    up = up_weight.transpose(0, 2, 1, 3).reshape(3, chans, 3 * deep).astype(F32)
    wu = jnp.concatenate([up[2], up[1] + up[2], up[0] + up[1], up[0]], axis=0).astype(BF16)
    w1 = conv_one.transpose(0, 2, 1, 3).reshape(3 * chans, 9 * chans)
    w2 = conv_two.transpose(0, 2, 1, 3).reshape(3 * chans, 9 * chans)
    vecs = jnp.stack([up_bias, gain_one, bias_one, gain_two, bias_two])
    vecs = jnp.broadcast_to(vecs[:, :, None], (5, chans, cols))
    vmem = pl.BlockSpec(memory_space=pltpu.VMEM)
    got = pl.pallas_call(
        functools.partial(body, slabs, tiles),
        out_shape=jax.ShapeDtypeStruct((frames, rows, chans, cols), BF16),
        in_specs=[vmem] * 5,
        out_specs=vmem,
        scratch_shapes=[
            pltpu.VMEM((2 * frames, 4, deep, cols), BF16),
            pltpu.VMEM((8, 4 * chans, cols), F32),
            pltpu.VMEM((frames, rows + 4, chans, cols), BF16),
            pltpu.VMEM((2 * frames, rows + 4, 3 * chans, cols), BF16),
            pltpu.VMEM((frames + 2, rows + 2, chans, cols), F32),
            pltpu.VMEM((frames + 2, rows + 2, 3 * chans, cols), BF16),
            pltpu.VMEM((frames, rows, chans, cols), F32),
            pltpu.SemaphoreType.DMA((2,)),
            pltpu.SemaphoreType.DMA((2,)),
            pltpu.SemaphoreType.DMA((frames,)),
            pltpu.SemaphoreType.DMA((frames,)),
            pltpu.SemaphoreType.DMA((frames, 2)),
            pltpu.SemaphoreType.DMA((frames, 2)),
        ],
        compiler_params=pltpu.CompilerParams(collective_id=0, has_side_effects=True, vmem_limit_bytes=48 * 2**20),
    )(packed, wu, w1, w2, vecs)
    return got.transpose(2, 0, 1, 3)


def solution(mesh):
    return jax.shard_map(
        functools.partial(shards, mesh.shape["slab"], mesh.shape["tile"]),
        mesh=mesh,
        in_specs=(P(None, "slab", "tile", None), P(), P(), P(), P(), P(), P(), P(), P()),
        out_specs=P(None, "slab", "tile", None),
        check_vma=False,
    )
```

profile of v0, /device:TPU:1, one launch (start us, length us, event | category | flops | bytes accessed | tf_op | source)
XLA Modules:
  0.0 70.3 jit_solution(9519955846758299592)
XLA Ops:
  0.0 1.1 %convert_bitcast_fusion = f32[3,96,3,192]{3,1,2,0:T(8,128)S(1)} fusion(bf16[3,3,96,192]{3,2,1,0:T(8,128)(2,1)} %param.10), kind=kLoop, calls=%fused_computation | loop fusion | flops 165888 | bytes 995328 | tf_op jit(solution)/shard_map/convert_element_type | solution.py:229
  1.1 0.2 copy.18
  1.3 0.2 copy.22
  1.5 0.1 add_convert_fusion.1
  1.5 0.2 copy.19
  1.7 0.2 copy.23
  1.8 0.2 copy.20
  2.0 0.2 copy.24
  2.2 0.2 copy.21
  2.3 0.2 copy.25
  2.5 0.9 %copy-done = bf16[3,3,96,288]{3,2,1,0:T(8,128)(2,1)S(1)} copy-done((bf16[3,3,96,288]{3,2,1,0:T(8,128)(2,1)S(1)}, bf16[3,3,96,288]{3,2,1,0:T(8,128)(2,1)}, u32[]{:S(2)}) %copy-start) | copy-done | bytes 497688
  3.4 0.5 copy.26
  3.9 0.6 reshape.23.w1
  4.5 0.5 copy-done.1
  5.0 0.5 copy.27
  5.5 0.6 reshape.24.w2
  6.0 0.5 copy-done.2
  6.5 0.3 copy.28.coarse
  6.8 0.4 copy-done.6
  7.1 0.0 copy-done.7
  7.2 0.3 copy-done.3
  7.5 0.1 broadcast_in_dim.2.vecs
  7.6 61.5 %shard_map.91 = bf16[4,8,96,128]{3,2,1,0:T(8,128)(2,1)S(1)} custom-call(bf16[4,2,192,128]{3,2,1,0:T(8,128)(2,1)S(1)} %copy.28.coarse, bf16[384,576]{1,0:T(8,128)(2,1)S(1)} %pad_maximum_fusion.wu, bf16[288,864]{1,0:T(8,128)(2,1)S(1)} %reshape.23.w1, bf16[288,864]{1,0:T(8,128)(2,1)S(1)} %reshape.24.w2, f32[5,96,128]{2,1,0:T(8,128)S(1)} %broadcast_in_dim.2.vecs), custom_call_target="tpu_custom_call" | custom-call | tf_op jit(solution)/shard_map/pallas_call | solution.py:236
  69.1 1.2 %copy.29 = bf16[96,4,8,128]{3,2,1,0:T(8,128)(2,1)} copy(bf16[96,4,8,128]{3,0,2,1:T(8,128)(2,1)S(1)} %bitcast.21) | data formatting | bytes 1572864 | tf_op jit(solution)/shard_map/transpose | solution.py:258
  (13 shorter events, 0.2 us)
Async XLA Ops:
  2.3 1.1 %copy-start = (bf16[3,3,96,288]{3,2,1,0:T(8,128)(2,1)S(1)}, bf16[3,3,96,288]{3,2,1,0:T(8,128)(2,1)}, u32[]{:S(2)}) copy-start(bf16[3,3,96,288]{3,2,1,0:T(8,128)(2,1)} %param.13) | copy-start | bytes 1492996
  3.9 1.1 %copy-start.1 = (bf16[3,3,96,288]{3,2,1,0:T(8,128)(2,1)S(1)}, bf16[3,3,96,288]{3,2,1,0:T(8,128)(2,1)}, u32[]{:S(2)}) copy-start(bf16[3,3,96,288]{3,2,1,0:T(8,128)(2,1)} %param.16) | copy-start | bytes 1492996
  5.4 1.0 %copy-start.2 = (bf16[192,4,4,64]{0,3,2,1:T(8,128)(2,1)S(1)}, bf16[192,4,4,64]{0,3,2,1:T(8,128)(2,1)}, u32[]{:S(2)}) copy-start(bf16[192,4,4,64]{0,3,2,1:T(8,128)(2,1)} %param.9) | copy-start | bytes 1179652
  6.5 0.7 copy-start.6
  6.5 0.7 copy-start.7
  6.8 0.7 copy-start.3
  6.8 0.7 copy-start.4
  6.8 0.7 copy-start.5
where the time goes:
time: 70.6 us; the launch traced here: 70.3 us
  Pallas kernels  61.5 us (87%)
  local copies, waits for them, and re-layouts  7.46 us (11%)
  other arithmetic  1.2 us (2%)
    pallas_call x1, Pallas kernels, shards(): pl.pallas_call(functools.partial(body, slabs, tiles), out_shape=jax.Shape...  61.5 us
    unnamed x16, local copies, waits for them, and re-layouts  2.54 us

commit v1 on v0

v1 whole, which is shorter than its diff:
```python
import functools

import jax
import jax.numpy as jnp
from jax import lax
from jax.experimental import pallas as pl
from jax.experimental.pallas import tpu as pltpu
from jax.sharding import PartitionSpec as P

MESH = pl.DeviceIdType.MESH
F32 = jnp.float32
BF16 = jnp.bfloat16


def body(slabs, tiles, coarse, up_w, one_w, two_w, up_b, one_g, one_b, two_g, two_b, out,
         cbuf, wu, w1, w2, vecs, spread, part, ups, x1, acc1, x2, acc2, near_send, near_recv, far_send, far_recv, hop_send, hop_recv):
    frames, _, _, cols = coarse.shape
    chans = out.shape[2]
    rows = out.shape[1]
    s = lax.axis_index("slab")
    t = lax.axis_index("tile")
    has_up, has_down = t > 0, t < tiles - 1
    has_prev, has_next = s > 0, s < slabs - 1
    sides = ((has_up, {"tile": t - 1}), (has_down, {"tile": t + 1}), (has_prev, {"slab": s - 1}), (has_next, {"slab": s + 1}))

    def remote(src, dst, send, recv, who):
        return pltpu.make_async_remote_copy(
            src_ref=src, dst_ref=dst, send_sem=send, recv_sem=recv, device_id=who, device_id_type=MESH)

    barrier = pltpu.get_barrier_semaphore()
    for there, who in sides:
        @pl.when(there)
        def _():
            pl.semaphore_signal(barrier, inc=1, device_id=who, device_id_type=MESH)
    pl.semaphore_wait(barrier, sum(there.astype(jnp.int32) for there, _ in sides))

    to_up = remote(coarse.at[:, 0], cbuf.at[pl.ds(frames, frames), 3], near_send.at[0], near_recv.at[0], {"tile": t - 1})
    to_down = remote(coarse.at[:, 1], cbuf.at[pl.ds(frames, frames), 0], near_send.at[1], near_recv.at[1], {"tile": t + 1})
    far = [remote(coarse.at[f], cbuf.at[f, pl.ds(1, 2)], far_send.at[f], far_recv.at[f], {"slab": s + 1}) for f in range(frames)]
    hop_up = [remote(cbuf.at[f, 1], cbuf.at[f, 3], hop_send.at[f, 0], hop_recv.at[f, 0], {"tile": t - 1}) for f in range(frames)]
    hop_down = [remote(cbuf.at[f, 2], cbuf.at[f, 0], hop_send.at[f, 1], hop_recv.at[f, 1], {"tile": t + 1}) for f in range(frames)]

    pl.when(has_up)(to_up.start)
    pl.when(has_down)(to_down.start)
    for f in reversed(range(frames)):
        pl.when(has_next)(far[f].start)

    for f in range(frames):
        cbuf[frames + f, 1] = coarse[f, 0]
        cbuf[frames + f, 2] = coarse[f, 1]

    rim = jnp.zeros(cbuf.shape[2:], BF16)

    @pl.when(jnp.logical_not(has_up))
    def _():
        for f in range(frames):
            cbuf[frames + f, 0] = rim

    @pl.when(jnp.logical_not(has_down))
    def _():
        for f in range(frames):
            cbuf[frames + f, 3] = rim

    @pl.when(jnp.logical_or(jnp.logical_not(has_prev), jnp.logical_not(has_up)))
    def _():
        for f in range(frames):
            cbuf[f, 0] = rim

    @pl.when(jnp.logical_or(jnp.logical_not(has_prev), jnp.logical_not(has_down)))
    def _():
        for f in range(frames):
            cbuf[f, 3] = rim

    @pl.when(jnp.logical_not(has_prev))
    def _():
        for f in range(frames):
            cbuf[f, 1] = rim
            cbuf[f, 2] = rim

    half = cols // 2
    lane = lax.broadcasted_iota(jnp.int32, (cols, cols), 0)
    col = lax.broadcasted_iota(jnp.int32, (cols, cols), 1)
    for j in range(2):
        hit = lane == j * half + lax.shift_right_arithmetic(col, 1)
        spread[:, j * cols:(j + 1) * cols] = jnp.where(hit, 1.0, 0.0).astype(BF16)

    for n, vec in enumerate((up_b, one_g, one_b, two_g, two_b)):
        vecs[n] = jnp.transpose(jnp.broadcast_to(vec[...], (cols, chans)))
    up = [jnp.concatenate([up_w[a, b] for b in range(3)], axis=1).astype(F32) for a in range(3)]
    for q, mix in enumerate((up[2], up[1] + up[2], up[0] + up[1], up[0])):
        wu[q * chans:(q + 1) * chans] = mix.astype(BF16)
    for raw, w in ((one_w, w1), (two_w, w2)):
        for tap in range(3):
            w[tap * chans:(tap + 1) * chans] = jnp.concatenate([raw[tap, a] for a in range(3)], axis=1)

    row_col = lax.broadcasted_iota(jnp.int32, (1, cols), 1)

    def norm_act(values, gain):
        meansq = jnp.mean(values * values, axis=0, keepdims=True)
        y = values * lax.rsqrt(meansq + 1e-06) * gain
        return y / (1.0 + jnp.exp(-y))

    def shifts(v):
        left = jnp.where(row_col == 0, 0.0, pltpu.roll(v, 1, 1)).astype(BF16)
        right = jnp.where(row_col == cols - 1, 0.0, pltpu.roll(v, cols - 1, 1)).astype(BF16)
        return left, v.astype(BF16), right

    def put(ref, f, r, act):
        pieces = shifts(act)

        def store():
            for b in range(3):
                ref[f, r, pl.ds(b * chans, chans)] = pieces[b]
        return store

    def run(trips, *steps, start=0):
        def trip(i, _):
            for store in [store for step in steps for store in step(i)]:
                store()
            return _
        lax.fori_loop(start, trips, trip, 0)

    top_keep = jnp.where(has_up, 1.0, 0.0)
    bottom_keep = jnp.where(has_down, 1.0, 0.0)
    past_keep = jnp.where(has_prev, 1.0, 0.0)

    def row_keep(r, low, high):
        return jnp.where(r < low, top_keep, jnp.where(r >= high, bottom_keep, 1.0))

    def expand(f):
        slot = f % 2

        def step(pair):
            wide = jnp.dot(cbuf[f, pair], spread[...], preferred_element_type=F32)
            near = [jnp.concatenate(shifts(wide[:, j * cols:(j + 1) * cols]), axis=0) for j in range(2)]
            got = jnp.dot(wu[...], jnp.concatenate(near, axis=1), preferred_element_type=F32)

            def store():
                part[slot, 2 * pair] = got[:, :cols]
                part[slot, 2 * pair + 1] = got[:, cols:]
            return [store]
        return step

    def finish(f, i):
        slot = f % 2
        even = part[slot, i, pl.ds(chans, chans)] + part[slot, i - 1, pl.ds(3 * chans, chans)]
        odd = part[slot, i, pl.ds(2 * chans, chans)] + part[slot, i + 1, pl.ds(0, chans)]
        stores = []
        for j, total in enumerate((even, odd)):
            r = 2 * (i - 1) + j
            value = (total + vecs[0]).astype(BF16)
            act = norm_act(value.astype(F32), vecs[1])
            keep = row_keep(r, 2, rows + 2)
            if f < frames:
                keep = keep * past_keep
            stores.append(put(x1, f, r, act * keep))
            if f >= frames:
                def keep_value(r=r, value=value):
                    ups[f - frames, r] = value
                stores.append(keep_value)
        return stores

    def finish_two(f):
        return lambda i: finish(f, i + 1) + finish(f, jnp.minimum(i + 5, 6))

    def conv(x, w, acc, f, last, start_of, done):
        taps = [tap for tap in range(3) if 0 <= f - tap <= last]
        lo, hi = taps[0], taps[-1] + 1

        def step(p):
            r = 2 * p
            lines = [x[f, r + a] for a in range(4)]
            rhs = jnp.concatenate([jnp.concatenate([lines[a], lines[a + 1]], axis=1) for a in range(3)], axis=0)
            got = jnp.dot(w[pl.ds(lo * chans, (hi - lo) * chans)], rhs, preferred_element_type=F32)

            def store():
                for tap in taps:
                    n = f - tap
                    for j in range(2):
                        mine = got[(tap - lo) * chans:(tap - lo + 1) * chans, j * cols:(j + 1) * cols]
                        total = mine + (start_of(n, r + j) if tap == 2 else acc[n, r + j])
                        if tap == 0 and done is not None:
                            done(n, r + j, total)
                        else:
                            acc[n, r + j] = total
            return [store]
        return step

    mids = frames + 2

    def conv_a(f):
        return conv(x1, w1, acc1, f, mids - 1, lambda n, r: vecs[2], None)

    def finished(n, r, total):
        out[n, r] = total.astype(BF16)

    def conv_b(f):
        return conv(x2, w2, acc2, f, frames - 1, lambda n, r: ups[n, r + 2].astype(F32) + vecs[4], finished)

    def second(n, r):
        act = norm_act(acc1[n, r], vecs[3])
        keep = row_keep(r, 1, rows + 1)
        if n < 2:
            keep = keep * past_keep
        return [put(x2, n, r, act * keep)]

    def second_two(n):
        return lambda p: second(n, 2 * p) + second(n, 2 * p + 1)

    newest = 2 * frames - 1
    run(3, expand(newest), start=1)
    pl.when(has_down)(to_up.wait_recv)
    pl.when(has_up)(to_down.wait_recv)

    def relay(f):
        @pl.when(has_prev)
        def _():
            far[f].wait_recv()
            pl.when(has_up)(hop_up[f].start)
            pl.when(has_down)(hop_down[f].start)

    def landed(f):
        @pl.when(has_prev)
        def _():
            pl.when(has_down)(hop_up[f].wait_recv)
            pl.when(has_up)(hop_down[f].wait_recv)

    run(1, expand(newest))
    run(4, expand(newest), start=3)
    wide_pairs = (rows + 2) // 2
    for f in reversed(range(2 * frames)):
        if 0 < f <= frames:
            landed(f - 1)
        if f > 0:
            run(4, finish_two(f), expand(f - 1))
        else:
            run(4, finish_two(f))
        if f >= frames:
            relay(f - frames)
        ready = f + 1
        if ready < mids:
            run(wide_pairs, second_two(ready), conv_a(f))
        else:
            run(wide_pairs, conv_a(f))
    run(wide_pairs, second_two(0))
    for f in reversed(range(mids)):
        run(rows // 2, conv_b(f))

    pl.when(has_up)(to_up.wait_send)
    pl.when(has_down)(to_down.wait_send)
    for f in range(frames):
        pl.when(has_next)(far[f].wait_send)
        pl.when(jnp.logical_and(has_prev, has_up))(hop_up[f].wait_send)
        pl.when(jnp.logical_and(has_prev, has_down))(hop_down[f].wait_send)


def shards(slabs, tiles, coarse, up_weight, up_bias, gain_one, conv_one, bias_one, gain_two, conv_two, bias_two):
    deep, frames, lines, half = coarse.shape
    chans = up_weight.shape[2]
    rows, cols = 2 * lines, 2 * half
    packed = coarse.transpose(1, 2, 0, 3).reshape(frames, lines // 2, 2, deep, half)
    packed = packed.transpose(0, 1, 3, 2, 4).reshape(frames, lines // 2, deep, cols)
    row = lambda vec: vec.reshape(1, chans)
    vmem = pl.BlockSpec(memory_space=pltpu.VMEM)
    got = pl.pallas_call(
        functools.partial(body, slabs, tiles),
        out_shape=jax.ShapeDtypeStruct((frames, rows, chans, cols), BF16),
        in_specs=[vmem] * 9,
        out_specs=vmem,
        scratch_shapes=[
            pltpu.VMEM((2 * frames, 4, deep, cols), BF16),
            pltpu.VMEM((4 * chans, 3 * deep), BF16),
            pltpu.VMEM((3 * chans, 9 * chans), BF16),
            pltpu.VMEM((3 * chans, 9 * chans), BF16),
            pltpu.VMEM((5, chans, cols), F32),
            pltpu.VMEM((cols, 2 * cols), BF16),
            pltpu.VMEM((2, 8, 4 * chans, cols), F32),
            pltpu.VMEM((frames, rows + 4, chans, cols), BF16),
            pltpu.VMEM((2 * frames, rows + 4, 3 * chans, cols), BF16),
            pltpu.VMEM((frames + 2, rows + 2, chans, cols), F32),
            pltpu.VMEM((frames + 2, rows + 2, 3 * chans, cols), BF16),
            pltpu.VMEM((frames, rows, chans, cols), F32),
            pltpu.SemaphoreType.DMA((2,)),
            pltpu.SemaphoreType.DMA((2,)),
            pltpu.SemaphoreType.DMA((frames,)),
            pltpu.SemaphoreType.DMA((frames,)),
            pltpu.SemaphoreType.DMA((frames, 2)),
            pltpu.SemaphoreType.DMA((frames, 2)),
        ],
        compiler_params=pltpu.CompilerParams(collective_id=0, has_side_effects=True, vmem_limit_bytes=48 * 2**20),
    )(packed, up_weight, conv_one, conv_two, row(up_bias), row(gain_one), row(bias_one), row(gain_two), row(bias_two))
    return got.transpose(2, 0, 1, 3)


def solution(mesh):
    return jax.shard_map(
        functools.partial(shards, mesh.shape["slab"], mesh.shape["tile"]),
        mesh=mesh,
        in_specs=(P(None, "slab", "tile", None), P(), P(), P(), P(), P(), P(), P(), P()),
        out_specs=P(None, "slab", "tile", None),
        check_vma=False,
    )
```

time: 70.6 us -> 49.9 us (0.71)
  Pallas kernels: 61.5 us -> 44.9 us
  local copies, waits for them, and re-layouts: 7.46 us -> 4.67 us
  other arithmetic: 1.2 us -> 0 us
    pallas_call x1, Pallas kernels: 61.5 us -> 44.9 us  [shards(): pl.pallas_call(functools.partial(body, slabs, tiles), out_shape=jax.Shape...]
    another operation x9 -> x0, local copies, waits for them, and re-layouts: 1.29 us -> none
    reshape x2 -> x0, local copies, waits for them, and re-layouts: 1.12 us -> none  [the longest x1 0.56 us: shards(): w2 = conv_two.transpose(0, 2, 1, 3).reshape(3 * chans, 9 * chans)]
    reshape x1, local copies, waits for them, and re-layouts: 0.26 us -> 1.36 us  [shards(): packed.transpose(0, 1, 3, 2, 4).reshape(frames, lines // 2, deep, cols)]
    convert_element_type x1 -> x0, other arithmetic: 1.08 us -> none  [shards(): up = up_weight.transpose(0, 2, 1, 3).reshape(3, chans, 3 * deep).astype(F32)]
    transpose x2 -> x0, local copies, waits for them, and re-layouts: 0.91 us -> none  [the longest x1 0.46 us: shards(): w1 = conv_one.transpose(0, 2, 1, 3).reshape(3 * chans, 9 * chans)]
where the time goes in v1:
time: 49.9 us; the launch traced here: 49.7 us
  Pallas kernels  44.9 us (90%)
  local copies, waits for them, and re-layouts  4.67 us (9%)
    pallas_call x1, Pallas kernels, shards(): pl.pallas_call(functools.partial(body, slabs, tiles), out_shape=jax.Shape...  44.9 us
    unnamed x16, local copies, waits for them, and re-layouts  2.12 us
    reshape x1, local copies, waits for them, and re-layouts, shards(): packed.transpose(0, 1, 3, 2, 4).reshape(frames, lines // 2, deep, cols)  1.36 us
    transpose x1, local copies, waits for them, and re-layouts, shards(): return got.transpose(2, 0, 1, 3)  1.19 us

profile of v1, /device:TPU:1, one launch (start us, length us, event | category | flops | bytes accessed | tf_op | source)
XLA Modules:
  0.0 49.7 jit_solution(1817559936284162279)
XLA Ops:
  0.0 0.0 copy-start
  0.0 0.0 copy-start.3
  0.0 0.0 copy-start.4
  0.0 0.0 copy-start.5
  0.0 0.0 copy-start.6
  0.0 0.0 copy-start.7
  0.0 1.4 %copy.12.coarse = bf16[4,2,192,128]{3,2,1,0:T(8,128)(2,1)S(1)} copy(bf16[4,2,192,128]{2,3,1,0:T(8,128)(2,1)} %bitcast.19) | data formatting | bytes 786432 | tf_op jit(solution)/shard_map/reshape | solution.py:262
  1.4 0.0 copy-done
  1.4 0.0 copy-done.3
  1.4 0.0 copy-done.4
  1.4 0.0 copy-done.5
  1.4 0.0 copy-done.6
  1.5 0.0 copy-done.7
  1.5 0.0 copy-start.1
  1.5 1.1 %copy-done.1 = bf16[3,3,96,288]{3,2,1,0:T(8,128)(2,1)S(1)} copy-done((bf16[3,3,96,288]{3,2,1,0:T(8,128)(2,1)S(1)}, bf16[3,3,96,288]{3,2,1,0:T(8,128)(2,1)}, u32[]{:S(2)}) %copy-start.1) | copy-done | bytes 497688
  2.6 0.0 copy-start.2
  2.6 1.0 %copy-done.2 = bf16[3,3,96,192]{3,2,1,0:T(8,128)(2,1)S(1)} copy-done((bf16[3,3,96,192]{3,2,1,0:T(8,128)(2,1)S(1)}, bf16[3,3,96,192]{3,2,1,0:T(8,128)(2,1)}, u32[]{:S(2)}) %copy-start.2) | copy-done | bytes 331800
  3.6 44.9 %shard_map.91 = bf16[4,8,96,128]{3,2,1,0:T(8,128)(2,1)S(1)} custom-call(bf16[4,2,192,128]{3,2,1,0:T(8,128)(2,1)S(1)} %copy.12.coarse, bf16[3,3,96,192]{3,2,1,0:T(8,128)(2,1)S(1)} %copy-done.2, bf16[3,3,96,288]{3,2,1,0:T(8,128)(2,1)S(1)} %copy-done, bf16[3,3,96,288]{3,2,1,0:T(8,128)(2,1)S(1)} %copy-done.1, f32[1,96]{1,0:T(1,128)S(1)} %bitcast.14, ...), custom_call_target="tpu_custom_call" | custom-call | tf_op jit(solution)/shard_map/pallas_call | solution.py:265
  48.5 1.2 %copy.13 = bf16[96,4,8,128]{3,2,1,0:T(8,128)(2,1)} copy(bf16[96,4,8,128]{3,0,2,1:T(8,128)(2,1)S(1)} %bitcast.13) | data formatting | bytes 1572864 | tf_op jit(solution)/shard_map/transpose | solution.py:292
Async XLA Ops:
  0.0 1.4 %copy-start = (bf16[3,3,96,288]{3,2,1,0:T(8,128)(2,1)S(1)}, bf16[3,3,96,288]{3,2,1,0:T(8,128)(2,1)}, u32[]{:S(2)}) copy-start(bf16[3,3,96,288]{3,2,1,0:T(8,128)(2,1)} %one_w.1) | copy-start | bytes 1492996
  0.0 1.4 %copy-start.3 = (f32[96]{0:T(128)S(1)}, f32[96]{0:T(128)}, u32[]{:S(2)}) copy-start(f32[96]{0:T(128)} %param.11) | copy-start | bytes 1156
  0.0 1.4 %copy-start.4 = (f32[96]{0:T(128)S(1)}, f32[96]{0:T(128)}, u32[]{:S(2)}) copy-start(f32[96]{0:T(128)} %param.12) | copy-start | bytes 1156
  0.0 1.4 %copy-start.5 = (f32[96]{0:T(128)S(1)}, f32[96]{0:T(128)}, u32[]{:S(2)}) copy-start(f32[96]{0:T(128)} %param.14) | copy-start | bytes 1156
  0.0 1.4 %copy-start.6 = (f32[96]{0:T(128)S(1)}, f32[96]{0:T(128)}, u32[]{:S(2)}) copy-start(f32[96]{0:T(128)} %param.15) | copy-start | bytes 1156
  0.0 1.4 %copy-start.7 = (f32[96]{0:T(128)S(1)}, f32[96]{0:T(128)}, u32[]{:S(2)}) copy-start(f32[96]{0:T(128)} %param.17) | copy-start | bytes 1156
  1.5 1.1 %copy-start.1 = (bf16[3,3,96,288]{3,2,1,0:T(8,128)(2,1)S(1)}, bf16[3,3,96,288]{3,2,1,0:T(8,128)(2,1)}, u32[]{:S(2)}) copy-start(bf16[3,3,96,288]{3,2,1,0:T(8,128)(2,1)} %two_w.1) | copy-start | bytes 1492996
  2.6 1.0 %copy-start.2 = (bf16[3,3,96,192]{3,2,1,0:T(8,128)(2,1)S(1)}, bf16[3,3,96,192]{3,2,1,0:T(8,128)(2,1)}, u32[]{:S(2)}) copy-start(bf16[3,3,96,192]{3,2,1,0:T(8,128)(2,1)} %up_w.1) | copy-start | bytes 995332

commit v2 on v1

--- a/solution.py
+++ b/solution.py
@@ -113,18 +113,20 @@
                 ref[f, r, pl.ds(b * chans, chans)] = pieces[b]
         return store
 
-    def run(trips, *steps, start=0):
+    def run(trips, *steps):
         def trip(i, _):
             for store in [store for step in steps for store in step(i)]:
                 store()
             return _
-        lax.fori_loop(start, trips, trip, 0)
+        lax.fori_loop(0, trips, trip, 0)
 
     top_keep = jnp.where(has_up, 1.0, 0.0)
     bottom_keep = jnp.where(has_down, 1.0, 0.0)
     past_keep = jnp.where(has_prev, 1.0, 0.0)
 
     def row_keep(r, low, high):
+        if isinstance(r, int):
+            return top_keep if r < low else bottom_keep if r >= high else 1.0
         return jnp.where(r < low, top_keep, jnp.where(r >= high, bottom_keep, 1.0))
 
     def expand(f):
@@ -133,11 +135,13 @@
         def step(pair):
             wide = jnp.dot(cbuf[f, pair], spread[...], preferred_element_type=F32)
             near = [jnp.concatenate(shifts(wide[:, j * cols:(j + 1) * cols]), axis=0) for j in range(2)]
-            got = jnp.dot(wu[...], jnp.concatenate(near, axis=1), preferred_element_type=F32)
+            lo = chans if pair == 0 else 0
+            hi = 3 * chans if pair == 3 else 4 * chans
+            got = jnp.dot(wu[lo:hi], jnp.concatenate(near, axis=1), preferred_element_type=F32)
 
             def store():
-                part[slot, 2 * pair] = got[:, :cols]
-                part[slot, 2 * pair + 1] = got[:, cols:]
+                part[slot, 2 * pair, lo:hi] = got[:, :cols]
+                part[slot, 2 * pair + 1, lo:hi] = got[:, cols:]
             return [store]
         return step
 
@@ -160,8 +164,15 @@
                 stores.append(keep_value)
         return stores
 
-    def finish_two(f):
-        return lambda i: finish(f, i + 1) + finish(f, jnp.minimum(i + 5, 6))
+    turns = ((1,), (2, 3), (4,), (5, 6))
+
+    def level(old, new):
+        for k in range(4):
+            stores = [store for i in turns[k] for store in finish(old, i)]
+            if new is not None:
+                stores += expand(new)(k)
+            for store in stores:
+                store()
 
     def conv(x, w, acc, f, last, start_of, done):
         taps = [tap for tap in range(3) if 0 <= f - tap <= last]
@@ -208,7 +219,12 @@
         return lambda p: second(n, 2 * p) + second(n, 2 * p + 1)
 
     newest = 2 * frames - 1
-    run(3, expand(newest), start=1)
+    def lone(pairs):
+        for pair in pairs:
+            for store in expand(newest)(pair):
+                store()
+
+    lone((1, 2))
     pl.when(has_down)(to_up.wait_recv)
     pl.when(has_up)(to_down.wait_recv)
 
@@ -225,16 +241,12 @@
             pl.when(has_down)(hop_up[f].wait_recv)
             pl.when(has_up)(hop_down[f].wait_recv)
 
-    run(1, expand(newest))
-    run(4, expand(newest), start=3)
+    lone((0, 3))
     wide_pairs = (rows + 2) // 2
     for f in reversed(range(2 * frames)):
         if 0 < f <= frames:
             landed(f - 1)
-        if f > 0:
-            run(4, finish_two(f), expand(f - 1))
-        else:
-            run(4, finish_two(f))
+        level(f, f - 1 if f > 0 else None)
         if f >= frames:
             relay(f - frames)
         ready = f + 1

time: 49.9 us -> 42.6 us (0.85)
  Pallas kernels: 44.9 us -> 37.6 us
    pallas_call x1, Pallas kernels: 44.9 us -> 37.6 us  [shards(): pl.pallas_call(functools.partial(body, slabs, tiles), out_shape=jax.Shape...]
where the time goes in v2:
time: 42.6 us; the launch traced here: 42.4 us
  Pallas kernels  37.6 us (88%)
  local copies, waits for them, and re-layouts  4.67 us (11%)
    pallas_call x1, Pallas kernels, shards(): pl.pallas_call(functools.partial(body, slabs, tiles), out_shape=jax.Shape...  37.6 us
    unnamed x16, local copies, waits for them, and re-layouts  2.12 us
    reshape x1, local copies, waits for them, and re-layouts, shards(): packed.transpose(0, 1, 3, 2, 4).reshape(frames, lines // 2, deep, cols)  1.36 us
    transpose x1, local copies, waits for them, and re-layouts, shards(): return got.transpose(2, 0, 1, 3)  1.19 us

profile of v2, /device:TPU:1, one launch (start us, length us, event | category | flops | bytes accessed | tf_op | source)
XLA Modules:
  0.0 42.4 jit_solution(5260617801141812584)
XLA Ops:
  0.0 0.0 copy-start
  0.0 0.0 copy-start.3
  0.0 0.0 copy-start.4
  0.0 0.0 copy-start.5
  0.0 0.0 copy-start.6
  0.0 0.0 copy-start.7
  0.0 1.4 %copy.12.coarse = bf16[4,2,192,128]{3,2,1,0:T(8,128)(2,1)S(1)} copy(bf16[4,2,192,128]{2,3,1,0:T(8,128)(2,1)} %bitcast.19) | data formatting | bytes 786432 | tf_op jit(solution)/shard_map/reshape | solution.py:274
  1.4 0.0 copy-done
  1.4 0.0 copy-done.3
  1.4 0.0 copy-done.4
  1.4 0.0 copy-done.5
  1.4 0.0 copy-done.6
  1.5 0.0 copy-done.7
  1.5 0.0 copy-start.1
  1.5 1.1 %copy-done.1 = bf16[3,3,96,288]{3,2,1,0:T(8,128)(2,1)S(1)} copy-done((bf16[3,3,96,288]{3,2,1,0:T(8,128)(2,1)S(1)}, bf16[3,3,96,288]{3,2,1,0:T(8,128)(2,1)}, u32[]{:S(2)}) %copy-start.1) | copy-done | bytes 497688
  2.6 0.0 copy-start.2
  2.6 1.0 %copy-done.2 = bf16[3,3,96,192]{3,2,1,0:T(8,128)(2,1)S(1)} copy-done((bf16[3,3,96,192]{3,2,1,0:T(8,128)(2,1)S(1)}, bf16[3,3,96,192]{3,2,1,0:T(8,128)(2,1)}, u32[]{:S(2)}) %copy-start.2) | copy-done | bytes 331800
  3.6 37.6 %shard_map.91 = bf16[4,8,96,128]{3,2,1,0:T(8,128)(2,1)S(1)} custom-call(bf16[4,2,192,128]{3,2,1,0:T(8,128)(2,1)S(1)} %copy.12.coarse, bf16[3,3,96,192]{3,2,1,0:T(8,128)(2,1)S(1)} %copy-done.2, bf16[3,3,96,288]{3,2,1,0:T(8,128)(2,1)S(1)} %copy-done, bf16[3,3,96,288]{3,2,1,0:T(8,128)(2,1)S(1)} %copy-done.1, f32[1,96]{1,0:T(1,128)S(1)} %bitcast.14, ...), custom_call_target="tpu_custom_call" | custom-call | tf_op jit(solution)/shard_map/pallas_call | solution.py:277
  41.2 1.2 %copy.13 = bf16[96,4,8,128]{3,2,1,0:T(8,128)(2,1)} copy(bf16[96,4,8,128]{3,0,2,1:T(8,128)(2,1)S(1)} %bitcast.13) | data formatting | bytes 1572864 | tf_op jit(solution)/shard_map/transpose | solution.py:304
Async XLA Ops:
  0.0 1.4 %copy-start = (bf16[3,3,96,288]{3,2,1,0:T(8,128)(2,1)S(1)}, bf16[3,3,96,288]{3,2,1,0:T(8,128)(2,1)}, u32[]{:S(2)}) copy-start(bf16[3,3,96,288]{3,2,1,0:T(8,128)(2,1)} %one_w.1) | copy-start | bytes 1492996
  0.0 1.4 %copy-start.3 = (f32[96]{0:T(128)S(1)}, f32[96]{0:T(128)}, u32[]{:S(2)}) copy-start(f32[96]{0:T(128)} %param.11) | copy-start | bytes 1156
  0.0 1.4 %copy-start.4 = (f32[96]{0:T(128)S(1)}, f32[96]{0:T(128)}, u32[]{:S(2)}) copy-start(f32[96]{0:T(128)} %param.12) | copy-start | bytes 1156
  0.0 1.4 %copy-start.5 = (f32[96]{0:T(128)S(1)}, f32[96]{0:T(128)}, u32[]{:S(2)}) copy-start(f32[96]{0:T(128)} %param.14) | copy-start | bytes 1156
  0.0 1.4 %copy-start.6 = (f32[96]{0:T(128)S(1)}, f32[96]{0:T(128)}, u32[]{:S(2)}) copy-start(f32[96]{0:T(128)} %param.15) | copy-start | bytes 1156
  0.0 1.4 %copy-start.7 = (f32[96]{0:T(128)S(1)}, f32[96]{0:T(128)}, u32[]{:S(2)}) copy-start(f32[96]{0:T(128)} %param.17) | copy-start | bytes 1156
  1.5 1.1 %copy-start.1 = (bf16[3,3,96,288]{3,2,1,0:T(8,128)(2,1)S(1)}, bf16[3,3,96,288]{3,2,1,0:T(8,128)(2,1)}, u32[]{:S(2)}) copy-start(bf16[3,3,96,288]{3,2,1,0:T(8,128)(2,1)} %two_w.1) | copy-start | bytes 1492996
  2.6 1.0 %copy-start.2 = (bf16[3,3,96,192]{3,2,1,0:T(8,128)(2,1)S(1)}, bf16[3,3,96,192]{3,2,1,0:T(8,128)(2,1)}, u32[]{:S(2)}) copy-start(bf16[3,3,96,192]{3,2,1,0:T(8,128)(2,1)} %up_w.1) | copy-start | bytes 995332

commit v3 on v2

--- a/solution.py
+++ b/solution.py
@@ -12,8 +12,8 @@
 BF16 = jnp.bfloat16
 
 
-def body(slabs, tiles, coarse, up_w, one_w, two_w, up_b, one_g, one_b, two_g, two_b, out,
-         cbuf, wu, w1, w2, vecs, spread, part, ups, x1, acc1, x2, acc2, near_send, near_recv, far_send, far_recv, hop_send, hop_recv):
+def body(slabs, tiles, coarse, up_hbm, one_hbm, two_hbm, up_b, one_g, one_b, two_g, two_b, out,
+         up_w, one_w, two_w, load, cbuf, wu, w1, w2, vecs, spread, part, ups, x1, acc1, x2, acc2, near_send, near_recv, far_send, far_recv, hop_send, hop_recv):
     frames, _, _, cols = coarse.shape
     chans = out.shape[2]
     rows = out.shape[1]
@@ -27,6 +27,11 @@
         return pltpu.make_async_remote_copy(
             src_ref=src, dst_ref=dst, send_sem=send, recv_sem=recv, device_id=who, device_id_type=MESH)
 
+    loads = [pltpu.make_async_copy(src, dst, load.at[n])
+             for n, (src, dst) in enumerate(((up_hbm, up_w), (one_hbm, one_w), (two_hbm, two_w)))]
+    for copy in loads:
+        copy.start()
+
     barrier = pltpu.get_barrier_semaphore()
     for there, who in sides:
         @pl.when(there)
@@ -86,13 +91,10 @@
 
     for n, vec in enumerate((up_b, one_g, one_b, two_g, two_b)):
         vecs[n] = jnp.transpose(jnp.broadcast_to(vec[...], (cols, chans)))
+    loads[0].wait()
     up = [jnp.concatenate([up_w[a, b] for b in range(3)], axis=1).astype(F32) for a in range(3)]
     for q, mix in enumerate((up[2], up[1] + up[2], up[0] + up[1], up[0])):
         wu[q * chans:(q + 1) * chans] = mix.astype(BF16)
-    for raw, w in ((one_w, w1), (two_w, w2)):
-        for tap in range(3):
-            w[tap * chans:(tap + 1) * chans] = jnp.concatenate([raw[tap, a] for a in range(3)], axis=1)
-
     row_col = lax.broadcasted_iota(jnp.int32, (1, cols), 1)
 
     def norm_act(values, gain):
@@ -225,6 +227,10 @@
                 store()
 
     lone((1, 2))
+    for copy, raw, w in ((loads[1], one_w, w1), (loads[2], two_w, w2)):
+        copy.wait()
+        for tap in range(3):
+            w[tap * chans:(tap + 1) * chans] = jnp.concatenate([raw[tap, a] for a in range(3)], axis=1)
     pl.when(has_down)(to_up.wait_recv)
     pl.when(has_up)(to_down.wait_recv)
 
@@ -274,12 +280,17 @@
     packed = packed.transpose(0, 1, 3, 2, 4).reshape(frames, lines // 2, deep, cols)
     row = lambda vec: vec.reshape(1, chans)
     vmem = pl.BlockSpec(memory_space=pltpu.VMEM)
+    hbm = pl.BlockSpec(memory_space=pltpu.HBM)
     got = pl.pallas_call(
         functools.partial(body, slabs, tiles),
         out_shape=jax.ShapeDtypeStruct((frames, rows, chans, cols), BF16),
-        in_specs=[vmem] * 9,
+        in_specs=[vmem] + [hbm] * 3 + [vmem] * 5,
         out_specs=vmem,
         scratch_shapes=[
+            pltpu.VMEM(up_weight.shape, BF16),
+            pltpu.VMEM(conv_one.shape, BF16),
+            pltpu.VMEM(conv_two.shape, BF16),
+            pltpu.SemaphoreType.DMA((3,)),
             pltpu.VMEM((2 * frames, 4, deep, cols), BF16),
             pltpu.VMEM((4 * chans, 3 * deep), BF16),
             pltpu.VMEM((3 * chans, 9 * chans), BF16),
@@ -299,7 +310,7 @@
             pltpu.SemaphoreType.DMA((frames, 2)),
             pltpu.SemaphoreType.DMA((frames, 2)),
         ],
-        compiler_params=pltpu.CompilerParams(collective_id=0, has_side_effects=True, vmem_limit_bytes=48 * 2**20),
+        compiler_params=pltpu.CompilerParams(collective_id=0, has_side_effects=True, vmem_limit_bytes=63950000),
     )(packed, up_weight, conv_one, conv_two, row(up_bias), row(gain_one), row(bias_one), row(gain_two), row(bias_two))
     return got.transpose(2, 0, 1, 3)
 

time: 42.6 us -> 44.1 us (1.035)
  Pallas kernels: 37.6 us -> 39.6 us
    unnamed x16 -> x0, local copies, waits for them, and re-layouts: 2.12 us -> none
    pallas_call x1, Pallas kernels: 37.6 us -> 39.6 us  [shards(): pl.pallas_call(functools.partial(body, slabs, tiles), out_shape=jax.Shape...]
    transpose x1, local copies, waits for them, and re-layouts: 1.19 us -> 2.32 us  [shards(): return got.transpose(2, 0, 1, 3)]
    reshape x1, local copies, waits for them, and re-layouts: 1.36 us -> 1.99 us  [shards(): packed.transpose(0, 1, 3, 2, 4).reshape(frames, lines // 2, deep, cols)]
where the time goes in v3:
time: 44.1 us; the launch traced here: 43.9 us
  Pallas kernels  39.6 us (90%)
  local copies, waits for them, and re-layouts  4.31 us (10%)
    pallas_call x1, Pallas kernels, shards(): pl.pallas_call(functools.partial(body, slabs, tiles), out_shape=jax.Shape...  39.6 us
    transpose x1, local copies, waits for them, and re-layouts, shards(): return got.transpose(2, 0, 1, 3)  2.32 us
    reshape x1, local copies, waits for them, and re-layouts, shards(): packed.transpose(0, 1, 3, 2, 4).reshape(frames, lines // 2, deep, cols)  1.99 us

profile of v3, /device:TPU:1, one launch (start us, length us, event | category | flops | bytes accessed | tf_op | source)
XLA Modules:
  0.0 43.9 jit_solution(2156924085712916566)
XLA Ops:
  0.0 2.0 %copy.12.coarse = bf16[4,2,192,128]{3,2,1,0:T(8,128)(2,1)} copy(bf16[4,2,192,128]{2,3,1,0:T(8,128)(2,1)} %bitcast.14) | data formatting | bytes 786432 | tf_op jit(solution)/shard_map/reshape | solution.py:280
  2.0 39.6 %shard_map.91 = bf16[4,8,96,128]{3,2,1,0:T(8,128)(2,1)} custom-call(bf16[4,2,192,128]{3,2,1,0:T(8,128)(2,1)} %copy.12.coarse, bf16[3,3,96,192]{3,2,1,0:T(8,128)(2,1)} %up_hbm.1, bf16[3,3,96,288]{3,2,1,0:T(8,128)(2,1)} %one_hbm.1, bf16[3,3,96,288]{3,2,1,0:T(8,128)(2,1)} %two_hbm.1, f32[1,96]{1,0:T(1,128)} %bitcast.15, f32[1,96]{1,0:T(1,128)} %bitcast.16, ...), custom_call_target="tpu_custom_call" | custom-call | tf_op jit(solution)/shard_map/pallas_call | solution.py:284
  41.6 2.3 %copy.13 = bf16[96,4,8,128]{3,2,1,0:T(8,128)(2,1)} copy(bf16[96,4,8,128]{3,0,2,1:T(8,128)(2,1)} %bitcast.13) | data formatting | bytes 1572864 | tf_op jit(solution)/shard_map/transpose | solution.py:315

commit v4 on v2

--- a/solution.py
+++ b/solution.py
@@ -114,11 +114,9 @@
         return store
 
     def run(trips, *steps):
-        def trip(i, _):
+        for i in range(trips):
             for store in [store for step in steps for store in step(i)]:
                 store()
-            return _
-        lax.fori_loop(0, trips, trip, 0)
 
     top_keep = jnp.where(has_up, 1.0, 0.0)
     bottom_keep = jnp.where(has_down, 1.0, 0.0)

time: 42.6 us -> 34.5 us (0.81)
  Pallas kernels: 37.6 us -> 29.5 us
    pallas_call x1, Pallas kernels: 37.6 us -> 29.5 us  [shards(): pl.pallas_call(functools.partial(body, slabs, tiles), out_shape=jax.Shape...]
where the time goes in v4:
time: 34.5 us; the launch traced here: 34.2 us
  Pallas kernels  29.5 us (86%)
  local copies, waits for them, and re-layouts  4.67 us (14%)
    pallas_call x1, Pallas kernels, shards(): pl.pallas_call(functools.partial(body, slabs, tiles), out_shape=jax.Shape...  29.5 us
    unnamed x16, local copies, waits for them, and re-layouts  2.12 us
    reshape x1, local copies, waits for them, and re-layouts, shards(): packed.transpose(0, 1, 3, 2, 4).reshape(frames, lines // 2, deep, cols)  1.36 us
    transpose x1, local copies, waits for them, and re-layouts, shards(): return got.transpose(2, 0, 1, 3)  1.19 us

profile of v4, /device:TPU:1, one launch (start us, length us, event | category | flops | bytes accessed | tf_op | source)
XLA Modules:
  0.0 34.2 jit_solution(14379342509825797779)
XLA Ops:
  0.0 0.0 copy-start
  0.0 0.0 copy-start.3
  0.0 0.0 copy-start.4
  0.0 0.0 copy-start.5
  0.0 0.0 copy-start.6
  0.0 0.0 copy-start.7
  0.0 1.4 %copy.12.coarse = bf16[4,2,192,128]{3,2,1,0:T(8,128)(2,1)S(1)} copy(bf16[4,2,192,128]{2,3,1,0:T(8,128)(2,1)} %bitcast.19) | data formatting | bytes 786432 | tf_op jit(solution)/shard_map/reshape | solution.py:272
  1.4 0.0 copy-done
  1.4 0.0 copy-done.3
  1.4 0.0 copy-done.4
  1.4 0.0 copy-done.5
  1.4 0.0 copy-done.6
  1.5 0.0 copy-done.7
  1.5 0.0 copy-start.1
  1.5 1.1 %copy-done.1 = bf16[3,3,96,288]{3,2,1,0:T(8,128)(2,1)S(1)} copy-done((bf16[3,3,96,288]{3,2,1,0:T(8,128)(2,1)S(1)}, bf16[3,3,96,288]{3,2,1,0:T(8,128)(2,1)}, u32[]{:S(2)}) %copy-start.1) | copy-done | bytes 497688
  2.6 0.0 copy-start.2
  2.6 1.0 %copy-done.2 = bf16[3,3,96,192]{3,2,1,0:T(8,128)(2,1)S(1)} copy-done((bf16[3,3,96,192]{3,2,1,0:T(8,128)(2,1)S(1)}, bf16[3,3,96,192]{3,2,1,0:T(8,128)(2,1)}, u32[]{:S(2)}) %copy-start.2) | copy-done | bytes 331800
  3.6 29.5 %shard_map.91 = bf16[4,8,96,128]{3,2,1,0:T(8,128)(2,1)S(1)} custom-call(bf16[4,2,192,128]{3,2,1,0:T(8,128)(2,1)S(1)} %copy.12.coarse, bf16[3,3,96,192]{3,2,1,0:T(8,128)(2,1)S(1)} %copy-done.2, bf16[3,3,96,288]{3,2,1,0:T(8,128)(2,1)S(1)} %copy-done, bf16[3,3,96,288]{3,2,1,0:T(8,128)(2,1)S(1)} %copy-done.1, f32[1,96]{1,0:T(1,128)S(1)} %bitcast.14, ...), custom_call_target="tpu_custom_call" | custom-call | tf_op jit(solution)/shard_map/pallas_call | solution.py:275
  33.1 1.2 %copy.13 = bf16[96,4,8,128]{3,2,1,0:T(8,128)(2,1)} copy(bf16[96,4,8,128]{3,0,2,1:T(8,128)(2,1)S(1)} %bitcast.13) | data formatting | bytes 1572864 | tf_op jit(solution)/shard_map/transpose | solution.py:302
Async XLA Ops:
  0.0 1.4 %copy-start = (bf16[3,3,96,288]{3,2,1,0:T(8,128)(2,1)S(1)}, bf16[3,3,96,288]{3,2,1,0:T(8,128)(2,1)}, u32[]{:S(2)}) copy-start(bf16[3,3,96,288]{3,2,1,0:T(8,128)(2,1)} %one_w.1) | copy-start | bytes 1492996
  0.0 1.4 %copy-start.3 = (f32[96]{0:T(128)S(1)}, f32[96]{0:T(128)}, u32[]{:S(2)}) copy-start(f32[96]{0:T(128)} %param.11) | copy-start | bytes 1156
  0.0 1.4 %copy-start.4 = (f32[96]{0:T(128)S(1)}, f32[96]{0:T(128)}, u32[]{:S(2)}) copy-start(f32[96]{0:T(128)} %param.12) | copy-start | bytes 1156
  0.0 1.4 %copy-start.5 = (f32[96]{0:T(128)S(1)}, f32[96]{0:T(128)}, u32[]{:S(2)}) copy-start(f32[96]{0:T(128)} %param.14) | copy-start | bytes 1156
  0.0 1.4 %copy-start.6 = (f32[96]{0:T(128)S(1)}, f32[96]{0:T(128)}, u32[]{:S(2)}) copy-start(f32[96]{0:T(128)} %param.15) | copy-start | bytes 1156
  0.0 1.4 %copy-start.7 = (f32[96]{0:T(128)S(1)}, f32[96]{0:T(128)}, u32[]{:S(2)}) copy-start(f32[96]{0:T(128)} %param.17) | copy-start | bytes 1156
  1.5 1.1 %copy-start.1 = (bf16[3,3,96,288]{3,2,1,0:T(8,128)(2,1)S(1)}, bf16[3,3,96,288]{3,2,1,0:T(8,128)(2,1)}, u32[]{:S(2)}) copy-start(bf16[3,3,96,288]{3,2,1,0:T(8,128)(2,1)} %two_w.1) | copy-start | bytes 1492996
  2.6 1.0 %copy-start.2 = (bf16[3,3,96,192]{3,2,1,0:T(8,128)(2,1)S(1)}, bf16[3,3,96,192]{3,2,1,0:T(8,128)(2,1)}, u32[]{:S(2)}) copy-start(bf16[3,3,96,192]{3,2,1,0:T(8,128)(2,1)} %up_w.1) | copy-start | bytes 995332
